TPU v7x, 256 devices: a whole 4x4x8 slice. The times are simulated.
256 devices in a mesh: snap: 64 (over x, y, z_hi), feat: 4 (over z_lo, core).
Axes of the slice: x: 4, y: 4, z: 8 (z_hi: 4, z_lo: 2; z = z_hi * 2 + z_lo), core: 2. Of those that a mesh axis runs over, the one named last changes fastest.
Arguments:
- features: bfloat16 [64, 2048, 1024], P('snap', None, 'feat'), may hold values from -6 to 6
- block_index: int32 [64, 16, 8], P('snap'), may hold values from 0 to 15
- block_values: bfloat16 [64, 16, 8, 128, 128], P('snap'), may hold values from -0.1875 to 0.1875
- hop_in: bfloat16 [1024, 1024], P(None, 'feat'), may hold values from -0.1875 to 0.1875
- query_w: bfloat16 [1024, 1024], P(None, 'feat'), may hold values from -0.1875 to 0.1875
- key_w: bfloat16 [1024, 1024], P(None, 'feat'), may hold values from -0.1875 to 0.1875
- value_w: bfloat16 [1024, 1024], P(None, 'feat'), may hold values from -0.1875 to 0.1875
- output_w: bfloat16 [1024, 1024], P(None, 'feat'), may hold values from -0.1875 to 0.1875
- hop_out: bfloat16 [1024, 1024], P(None, 'feat'), may hold values from -0.1875 to 0.1875
- time_bias: float32 [64, 64], replicated, may hold values from -2 to 403
Outputs:
- result: bfloat16 [64, 2048, 1024], P('snap', None, 'feat')
All inputs are finite; a program needn't handle non-finite values.
Results may differ from a plain program's by a relative error of at most 0.012.
Values may be sent and summed in bfloat16 or wider, within the bound.
No kernel may reach another device: no remote copies, remote signals or barrier semaphores. Data moves between devices by JAX's collectives and lax.ppermute only.
A program may use at most 64 MiB of HBM per device.

v0:
```python
import math

import jax
import jax.numpy as jnp
from jax import lax
from jax.experimental import pallas as pl
from jax.experimental.pallas import tpu as pltpu
from jax.sharding import Mesh
from jax.sharding import PartitionSpec as P


VERT, FEAT, BLK, NBR, SNAPS = 2048, 1024, 128, 8, 64
ROWS = VERT // BLK
GROUP = 4
COLS = FEAT // GROUP
DEVS = SNAPS * GROUP
HALF = FEAT // 2
QUART = FEAT // 4
OWN = VERT // DEVS
LOCAL = SNAPS * OWN
AXES = ("x", "y", "zh", "zl", "core")
ORDER = ("zl", "core", "x", "y", "zh")
F32, BF16 = jnp.float32, jnp.bfloat16
STEP = 8


def hop_body(relu, index, field, blocks, out):
    step = pl.program_id(0)
    for i in range(STEP):
        picked, left = [], []
        for k in range(NBR):
            start = pl.multiple_of(index[k, step * STEP + i] * BLK, BLK)
            picked.append(field[pl.ds(start, BLK), :])
            left.append(blocks[i, k])
        total = jnp.dot(
            jnp.concatenate(left, axis=1),
            jnp.concatenate(picked, axis=0),
            preferred_element_type=F32,
        )
        if relu:
            total = jnp.maximum(total, 0.0)
        out[i * BLK : (i + 1) * BLK, :] = total.astype(BF16)


def hop(field, index, blocks, relu):
    def body(*refs):
        hop_body(relu, *refs)

    return pl.pallas_call(
        body,
        out_shape=jax.ShapeDtypeStruct((VERT, COLS), BF16),
        grid_spec=pltpu.PrefetchScalarGridSpec(
            num_scalar_prefetch=1,
            grid=(ROWS // STEP,),
            in_specs=[
                pl.BlockSpec((VERT, COLS), lambda r, ix: (0, 0)),
                pl.BlockSpec((STEP, NBR, BLK, BLK), lambda r, ix: (r, 0, 0, 0)),
            ],
            out_specs=pl.BlockSpec((STEP * BLK, COLS), lambda r, ix: (r, 0)),
        ),
        name="hop_relu" if relu else "hop",
    )(index, field, blocks)


def middle_body(scale, own, bias, got, *refs):
    pieces, out = refs[:24], refs[24]
    w, hidden, query, keys, values, table, sems = refs[25:]
    me = own[0]
    copies = []
    for i in range(6):
        group, j = i // 3, i % 3
        half = own[1 + group]
        row = []

        def move(piece, block, start=None):
            place = w.at[i, jnp.bitwise_xor(me, block)]
            if start is not None:
                place = place.at[pl.ds(pl.multiple_of(start, QUART), QUART)]
            row.append(pltpu.make_async_copy(piece, place, sems.at[i, len(row)]))

        move(pieces[i], 0)
        move(pieces[6 + i], 1)
        for g in range(2):
            far, *sides = pieces[12 + group * 6 + g * 3 : 15 + group * 6 + g * 3]
            for sub in range(2):
                move(far.at[sub, j], 2 + g, half * HALF + sub * QUART)
                move(sides[sub].at[j], 2 + g, (1 - half) * HALF + sub * QUART)
        copies.append(row)
    for row in copies:
        for copy in row:
            copy.start()

    def block(g):
        return slice(g * COLS, (g + 1) * COLS)

    def dot(a, b):
        return jnp.dot(a, b, preferred_element_type=F32)

    def arrive(i):
        for copy in copies[i]:
            copy.wait()

    rest, spread = bias[...], None
    at = lax.broadcasted_iota(jnp.int32, (LOCAL, SNAPS), 0) // OWN
    onehot = (at == lax.broadcasted_iota(jnp.int32, (LOCAL, SNAPS), 1)).astype(F32).astype(BF16)
    for _ in range(3):
        part = rest.astype(BF16)
        rest = rest - part.astype(F32)
        rows = dot(onehot, part).astype(BF16)
        part = lax.dot_general(rows, onehot, (((1,), (1,)), ((), ())), preferred_element_type=F32)
        spread = part if spread is None else spread + part
    vertex = lax.broadcasted_iota(jnp.int32, (LOCAL, LOCAL), 0) % OWN
    other = lax.broadcasted_iota(jnp.int32, (LOCAL, LOCAL), 1) % OWN
    table[...] = jnp.where(vertex == other, spread, -jnp.inf)

    agg = jnp.concatenate([got[g] for g in range(4)], axis=1)
    arrive(0)
    for g in range(4):
        hidden[:, block(g)] = jnp.maximum(dot(agg, w[0, g]), 0.0).astype(BF16)
    for i, ref in ((1, query), (2, keys), (3, values)):
        arrive(i)
        for g in range(4):
            ref[:, block(g)] = dot(hidden[...], w[i, g]).astype(BF16)
    logits = (
        lax.dot_general(query[...], keys[...], (((1,), (1,)), ((), ())), preferred_element_type=F32)
        * scale
        + table[...]
    )
    weights = jnp.exp(logits - jnp.max(logits, axis=1, keepdims=True))
    probs = (weights / jnp.sum(weights, axis=1, keepdims=True)).astype(BF16)
    for g in range(4):
        query[:, block(g)] = dot(probs, values[:, block(g)]).astype(BF16)
    arrive(4)
    for g in range(4):
        update = dot(query[...], w[4, g])
        keys[:, block(g)] = (hidden[:, block(g)].astype(F32) + update).astype(BF16)
    arrive(5)
    for g in range(4):
        out[g] = dot(keys[...], w[5, g]).astype(BF16)


def middle(own, bias, got, pieces, scale):
    def body(*refs):
        middle_body(scale, *refs)

    vmem = pl.BlockSpec(memory_space=pltpu.VMEM)
    return pl.pallas_call(
        body,
        out_shape=jax.ShapeDtypeStruct((GROUP, LOCAL, COLS), BF16),
        in_specs=[pl.BlockSpec(memory_space=pltpu.SMEM), vmem, vmem]
        + [pl.BlockSpec(memory_space=pl.ANY)] * 24,
        out_specs=vmem,
        scratch_shapes=[pltpu.VMEM((6, GROUP, FEAT, COLS), BF16)]
        + [pltpu.VMEM((LOCAL, FEAT), BF16)] * 4
        + [pltpu.VMEM((LOCAL, LOCAL), F32), pltpu.SemaphoreType.DMA((6, 10))],
        name="middle",
    )(own, bias, got, *pieces)


def pack_body(half, *refs):
    inputs, outputs, sems = refs[:6], refs[6:8], refs[8]
    copies = []
    for i in range(6):
        start = half[i // 3] * HALF
        for sub in range(2):
            rows = pl.ds(pl.multiple_of(start + sub * QUART, QUART), QUART)
            place = outputs[i // 3].at[sub, i % 3]
            copies.append(pltpu.make_async_copy(inputs[i].at[rows], place, sems.at[i, sub]))
    for copy in copies:
        copy.start()
    for copy in copies:
        copy.wait()


def pack(half, weights):
    anywhere = pl.BlockSpec(memory_space=pl.ANY)
    return pl.pallas_call(
        pack_body,
        out_shape=[jax.ShapeDtypeStruct((2, 3, QUART, COLS), BF16)] * 2,
        in_specs=[pl.BlockSpec(memory_space=pltpu.SMEM)] + [anywhere] * 6,
        out_specs=[pl.BlockSpec(memory_space=pltpu.VMEM)] * 2,
        scratch_shapes=[pltpu.SemaphoreType.DMA((6, 2))],
        name="pack",
    )(half, *weights)


def z_partner(up):
    pairs = []
    for zh in range(4):
        for zl in range(2):
            z = zh * 2 + zl
            there = (z + (1 if up else -1)) % 8
            pairs.append((z, there))
    return pairs


def local(features, block_index, block_values, hop_in, query_w, key_w, value_w, output_w, hop_out, time_bias):
    scale = 1.0 / math.sqrt(FEAT)
    weights = (hop_in, query_w, key_w, value_w, output_w, hop_out)
    swap = [(0, 1), (1, 0)]
    halves = jnp.stack([lax.axis_index("x") % 2, lax.axis_index("y") % 2]).astype(jnp.int32)
    groups = pack(halves, weights)
    features, groups = lax.optimization_barrier((features, groups))
    far = []
    for g in range(2):
        far.append(lax.ppermute(groups[g], ("zh", "zl"), z_partner(g == 1)))
    swapped = [lax.ppermute(w, "core", swap) for w in weights]
    far, swapped = lax.optimization_barrier((far, swapped))
    pieces = list(weights) + list(swapped)
    even, odd = [(0, 1), (1, 0), (2, 3), (3, 2)], [(0, 3), (3, 0), (1, 2), (2, 1)]
    for g in range(2):
        sides = []
        for sub in range(2):
            sides.append(lax.ppermute(far[g][sub], "xy"[g], (even, odd)[sub]))
        far_swap = lax.ppermute(far[g], "core", swap)
        side_swap = [lax.ppermute(side, "core", swap) for side in sides]
        pieces += [far[g], *sides, far_swap, *side_swap]
    index = block_index[0].T
    blocks = block_values[0]
    place = lax.axis_index("zl") * 2 + lax.axis_index("core")
    own = jnp.concatenate([place.astype(jnp.int32).reshape(1), halves])

    agg = hop(features[0], index, blocks, False)
    got = lax.all_to_all(agg.reshape(DEVS, OWN, COLS), ORDER, 0, 0, tiled=True)
    sent = middle(own, time_bias, got.reshape(GROUP, LOCAL, COLS), pieces, scale)
    back = lax.all_to_all(sent.reshape(DEVS, OWN, COLS), ORDER, 0, 0, tiled=True)
    return hop(back.reshape(VERT, COLS), index, blocks, True)[None]


def solution(mesh):
    fine = Mesh(mesh.devices.reshape(4, 4, 4, 2, 2), AXES)
    snap, feat = ("x", "y", "zh"), ("zl", "core")
    in_specs = (
        P(snap, None, feat),
        P(snap, None, None),
        P(snap, None, None, None, None),
    ) + (P(None, feat),) * 6 + (P(),)

    return jax.shard_map(
        local, mesh=fine, in_specs=in_specs, out_specs=P(snap, None, feat), check_vma=False
    )
```

profile of v0, /device:TPU:1, one launch (start us, length us, event | category | flops | bytes accessed | tf_op | source)
XLA Modules:
  0.0 118.1 jit_solution(11915216951606526143)
XLA Ops:
  0.0 3.2 %collective-permute-start.2 = (bf16[1024,256]{1,0:T(8,128)(2,1)}, bf16[1024,256]{1,0:T(8,128)(2,1)}, u32[]{:S(2)}, u32[]{:S(2)}) collective-permute-start(bf16[1024,256]{1,0:T(8,128)(2,1)} %refs_3_.3), channel_id=1, source_target_pairs={{0,1},{1,0},{2,3},{3,2},{4,5},{5,4},{6,7},{7,6},{8,9},{9,8},{10,11... | collective-permute-start | bytes 1572872 | tf_op jit(solution)/shard_map/ppermute | solution.py:207
  3.2 0.0 collective-permute-start.3
  3.2 0.5 collective-permute-start.4
  3.7 0.6 pad_add_fusion.1.half
  4.3 3.4 %pack.1 = (bf16[2,3,256,256]{3,2,1,0:T(8,128)(2,1)}, bf16[2,3,256,256]{3,2,1,0:T(8,128)(2,1)}) custom-call(s32[2]{0:T(128)} %pad_add_fusion.1.half, bf16[1024,256]{1,0:T(8,128)(2,1)} %refs_3_.3, bf16[1024,256]{1,0:T(8,128)(2,1)} %refs_4_.3, bf16[1024,256]{1,0:T(8,128)(2,1)} %refs_5_.3, bf16[1024,256]{1,0:T(8,128)(2,1)} %refs_6_.1, ...), custom_call_target="tpu_custom_call" | custom-call | tf_op jit(solution)/shard_map/pack/pallas_call | solution.py:177
  7.7 3.9 %collective-permute-start = (bf16[2,3,256,256]{3,2,1,0:T(8,128)(2,1)}, bf16[2,3,256,256]{3,2,1,0:T(8,128)(2,1)S(1)}, u32[]{:S(2)}, u32[]{:S(2)}) collective-permute-start(bf16[2,3,256,256]{3,2,1,0:T(8,128)(2,1)} %get-tuple-element.21), channel_id=1, source_target_pairs={{0,14},{2,0},{4,2},{6,4},{8,6},{10,8},{12,10},{14,12},{1,15},{3,1}... | collective-permute-start | bytes 2359304 | tf_op jit(solution)/shard_map/ppermute | solution.py:206
  11.6 0.0 collective-permute-start.1
  11.6 0.0 copy-start.3
  11.6 5.0 %hop.1 = bf16[2048,256]{1,0:T(8,128)(2,1)} custom-call(s32[8,16]{1,0:T(8,128)} %bitcast.28, bf16[2048,256]{1,0:T(8,128)(2,1)} %bitcast.27, bf16[16,8,128,128]{3,2,1,0:T(8,128)(2,1)} %bitcast.21), custom_call_target="tpu_custom_call" | custom-call | tf_op jit(solution)/shard_map/hop/pallas_call | solution.py:49
  16.7 10.6 %all-to-all-start = ((bf16[256,8,256]{2,1,0:T(8,128)(2,1)}), bf16[256,8,256]{2,1,0:T(8,128)(2,1)S(1)}, u32[]{:S(2)}, u32[]{:S(2)}) async-start(bf16[256,8,256]{2,1,0:T(8,128)(2,1)} %bitcast.25), calls=%async_computation | async-start | bytes 2097152 | tf_op jit(solution)/shard_map/all_to_all | solution.py:224
  27.3 0.0 collective-permute-done.2.refs_9_
  27.3 0.0 copy-done.3
  27.3 2.2 %collective-permute-start.5 = (bf16[1024,256]{1,0:T(8,128)(2,1)S(1)}, bf16[1024,256]{1,0:T(8,128)(2,1)S(1)}, u32[]{:S(2)}, u32[]{:S(2)}) collective-permute-start(bf16[1024,256]{1,0:T(8,128)(2,1)S(1)} %copy-done.3), channel_id=1, source_target_pairs={{0,1},{1,0},{2,3},{3,2},{4,5},{5,4},{6,7},{7,6},{8,9},{9,8},{10,11... | collective-permute-start | bytes 1572872 | tf_op jit(solution)/shard_map/ppermute | solution.py:207
  29.5 0.0 collective-permute-done.3.refs_10_
  29.5 0.1 collective-permute-start.6
  29.6 0.0 collective-permute-done.4.refs_11_
  29.6 0.4 collective-permute-start.7
  30.0 1.0 collective-permute-done.5.refs_12_
  31.1 0.0 copy-start.5
  31.1 0.7 collective-permute-done.6.refs_13_
  31.8 0.0 copy-start.6
  31.8 0.7 collective-permute-done.7.refs_14_
  32.6 0.0 copy-start.7
  32.6 0.0 collective-permute-done.refs_15_
  32.6 0.0 copy-done.5
  32.6 0.1 copy-done.6
  32.6 0.7 copy-done.7
  33.3 0.0 copy-start.1
  33.4 0.0 collective-permute-done.1.refs_21_
  33.4 0.0 copy-start.2
  33.4 0.1 slice_bitcast_fusion.2
  33.4 0.1 collective-permute-start.8
  33.5 4.1 %collective-permute-start.10 = (bf16[2,3,256,256]{3,2,1,0:T(8,128)(2,1)S(1)}, bf16[2,3,256,256]{3,2,1,0:T(8,128)(2,1)S(1)}, u32[]{:S(2)}, u32[]{:S(2)}) collective-permute-start(bf16[2,3,256,256]{3,2,1,0:T(8,128)(2,1)S(1)} %collective-permute-done.refs_15_), channel_id=1, source_target_pairs={{0,1},{1,0},{2,3},{3,2},{4,5},{5,4},{6,7},{7,6},{8,9},{9,8},{10,11... | collective-permute-start | bytes 2359304 | tf_op jit(solution)/shard_map/ppermute | solution.py:215
  37.7 1.8 %collective-permute-start.9 = (bf16[3,256,256]{2,1,0:T(8,128)(2,1)S(1)}, bf16[3,256,256]{2,1,0:T(8,128)(2,1)}, u32[]{:S(2)}, u32[]{:S(2)}) collective-permute-start(bf16[3,256,256]{2,1,0:T(8,128)(2,1)S(1)} %get-tuple-element.33), channel_id=1, source_target_pairs={{0,192},{192,0},{64,128},{128,64},{1,193},{193,1},{65,129},{129,65... | collective-permute-start | bytes 1179656 | tf_op jit(solution)/shard_map/ppermute | solution.py:214
  39.4 0.1 slice_bitcast_fusion
  39.5 1.4 %collective-permute-start.13 = (bf16[3,256,256]{2,1,0:T(8,128)(2,1)S(1)}, bf16[3,256,256]{2,1,0:T(8,128)(2,1)}, u32[]{:S(2)}, u32[]{:S(2)}) collective-permute-start(bf16[3,256,256]{2,1,0:T(8,128)(2,1)S(1)} %get-tuple-element.32), channel_id=1, source_target_pairs={{0,16},{16,0},{32,48},{48,32},{1,17},{17,1},{33,49},{49,33},{2,18}... | collective-permute-start | bytes 1179656 | tf_op jit(solution)/shard_map/ppermute | solution.py:214
  40.9 1.9 %collective-permute-start.14 = (bf16[3,256,256]{2,1,0:T(8,128)(2,1)S(1)}, bf16[3,256,256]{2,1,0:T(8,128)(2,1)}, u32[]{:S(2)}, u32[]{:S(2)}) collective-permute-start(bf16[3,256,256]{2,1,0:T(8,128)(2,1)S(1)} %get-tuple-element.31), channel_id=1, source_target_pairs={{0,48},{48,0},{16,32},{32,16},{1,49},{49,1},{17,33},{33,17},{2,50}... | collective-permute-start | bytes 1179656 | tf_op jit(solution)/shard_map/ppermute | solution.py:214
  42.8 5.3 %collective-permute-done.8.refs_16_ = bf16[3,256,256]{2,1,0:T(8,128)(2,1)} collective-permute-done((bf16[3,256,256]{2,1,0:T(8,128)(2,1)S(1)}, bf16[3,256,256]{2,1,0:T(8,128)(2,1)}, u32[]{:S(2)}, u32[]{:S(2)}) %collective-permute-start.8) | collective-permute-done | bytes 393248 | tf_op jit(solution)/shard_map/ppermute | solution.py:214
  48.1 3.8 %collective-permute-start.15 = (bf16[2,3,256,256]{3,2,1,0:T(8,128)(2,1)S(1)}, bf16[2,3,256,256]{3,2,1,0:T(8,128)(2,1)}, u32[]{:S(2)}, u32[]{:S(2)}) collective-permute-start(bf16[2,3,256,256]{3,2,1,0:T(8,128)(2,1)S(1)} %collective-permute-done.1.refs_21_), channel_id=1, source_target_pairs={{0,1},{1,0},{2,3},{3,2},{4,5},{5,4},{6,7},{7,6},{8,9},{9,8},{10,11... | collective-permute-start | bytes 2359304 | tf_op jit(solution)/shard_map/ppermute | solution.py:215
  51.9 3.6 %collective-permute-done.9.refs_17_ = bf16[3,256,256]{2,1,0:T(8,128)(2,1)} collective-permute-done((bf16[3,256,256]{2,1,0:T(8,128)(2,1)S(1)}, bf16[3,256,256]{2,1,0:T(8,128)(2,1)}, u32[]{:S(2)}, u32[]{:S(2)}) %collective-permute-start.9) | collective-permute-done | bytes 393248 | tf_op jit(solution)/shard_map/ppermute | solution.py:214
  55.5 0.6 collective-permute-start.11
  56.1 0.0 collective-permute-done.13.refs_22_
  56.1 0.4 collective-permute-start.12
  56.5 1.4 %collective-permute-done.14.refs_23_ = bf16[3,256,256]{2,1,0:T(8,128)(2,1)} collective-permute-done((bf16[3,256,256]{2,1,0:T(8,128)(2,1)S(1)}, bf16[3,256,256]{2,1,0:T(8,128)(2,1)}, u32[]{:S(2)}, u32[]{:S(2)}) %collective-permute-start.14) | collective-permute-done | bytes 393248 | tf_op jit(solution)/shard_map/ppermute | solution.py:214
  58.0 1.0 collective-permute-start.16
  59.0 0.0 collective-permute-done.10.refs_18_
  59.0 0.0 copy-start.4
  59.0 0.3 collective-permute-start.17
  59.2 0.6 pad_add_fusion.refs_0_
  59.8 0.0 collective-permute-done.11.refs_19_
  59.8 0.0 collective-permute-done.12.refs_20_
  59.8 0.0 collective-permute-done.15.refs_24_
  59.8 0.8 collective-permute-done.16.refs_25_
  60.6 0.6 collective-permute-done.17.refs_26_
  61.2 0.0 all-to-all-done
  61.2 0.0 copy-start
  61.2 0.0 copy-done.1
  61.2 0.0 copy-done.2
  61.2 0.0 copy-done.4
  61.2 1.0 copy-done
  62.2 13.2 %middle.1 = bf16[4,512,256]{2,1,0:T(8,128)(2,1)} custom-call(s32[3]{0:T(128)} %pad_add_fusion.refs_0_, f32[64,64]{1,0:T(8,128)} %refs_1_.3, bf16[4,512,256]{2,1,0:T(8,128)(2,1)} %bitcast.23, bf16[1024,256]{1,0:T(8,128)(2,1)} %refs_3_.3, bf16[1024,256]{1,0:T(8,128)(2,1)} %refs_4_.3, bf16[1024,256]{1,0:T(8,128)(2,1)} %refs_5_.3, bf16[1024,256]{1,0:T(8,128)(2,1)} %refs_6_.1, ...), custom_call_target="tpu_custom_call" | custom-call | tf_op jit(solution)/shard_map/middle/pallas_call | solution.py:147
  75.4 37.7 %all_to_all.10 = bf16[256,8,256]{2,1,0:T(8,128)(2,1)} all-to-all(bf16[256,8,256]{2,1,0:T(8,128)(2,1)} %bitcast.24), channel_id=1, replica_groups=mesh['x'=4,'y'=4,'zh'=4,'zl'=2,'core'=2] {'zl','core','x','y','zh'}, dimensions={0} | all-to-all | bytes 2097152 | tf_op jit(solution)/shard_map/all_to_all | solution.py:226
  113.1 4.9 %hop_relu.1 = bf16[2048,256]{1,0:T(8,128)(2,1)} custom-call(s32[8,16]{1,0:T(8,128)} %bitcast.29, bf16[2048,256]{1,0:T(8,128)(2,1)} %bitcast.26, bf16[16,8,128,128]{3,2,1,0:T(8,128)(2,1)} %bitcast.22), custom_call_target="tpu_custom_call" | custom-call | tf_op jit(solution)/shard_map/hop_relu/pallas_call | solution.py:49
Async XLA Ops:
  0.0 27.3 %collective-permute-start.2 = (bf16[1024,256]{1,0:T(8,128)(2,1)}, bf16[1024,256]{1,0:T(8,128)(2,1)}, u32[]{:S(2)}, u32[]{:S(2)}) collective-permute-start(bf16[1024,256]{1,0:T(8,128)(2,1)} %refs_3_.3), channel_id=1, source_target_pairs={{0,1},{1,0},{2,3},{3,2},{4,5},{5,4},{6,7},{7,6},{8,9},{9,8},{10,11... | collective-permute-start | bytes 1572872 | tf_op jit(solution)/shard_map/ppermute | solution.py:207
  3.2 26.3 %collective-permute-start.3 = (bf16[1024,256]{1,0:T(8,128)(2,1)}, bf16[1024,256]{1,0:T(8,128)(2,1)}, u32[]{:S(2)}, u32[]{:S(2)}) collective-permute-start(bf16[1024,256]{1,0:T(8,128)(2,1)} %refs_4_.3), channel_id=1, source_target_pairs={{0,1},{1,0},{2,3},{3,2},{4,5},{5,4},{6,7},{7,6},{8,9},{9,8},{10,11... | collective-permute-start | bytes 1572872 | tf_op jit(solution)/shard_map/ppermute | solution.py:207
  3.2 26.4 %collective-permute-start.4 = (bf16[1024,256]{1,0:T(8,128)(2,1)}, bf16[1024,256]{1,0:T(8,128)(2,1)}, u32[]{:S(2)}, u32[]{:S(2)}) collective-permute-start(bf16[1024,256]{1,0:T(8,128)(2,1)} %refs_5_.3), channel_id=1, source_target_pairs={{0,1},{1,0},{2,3},{3,2},{4,5},{5,4},{6,7},{7,6},{8,9},{9,8},{10,11... | collective-permute-start | bytes 1572872 | tf_op jit(solution)/shard_map/ppermute | solution.py:207
  7.7 24.9 %collective-permute-start = (bf16[2,3,256,256]{3,2,1,0:T(8,128)(2,1)}, bf16[2,3,256,256]{3,2,1,0:T(8,128)(2,1)S(1)}, u32[]{:S(2)}, u32[]{:S(2)}) collective-permute-start(bf16[2,3,256,256]{3,2,1,0:T(8,128)(2,1)} %get-tuple-element.21), channel_id=1, source_target_pairs={{0,14},{2,0},{4,2},{6,4},{8,6},{10,8},{12,10},{14,12},{1,15},{3,1}... | collective-permute-start | bytes 2359304 | tf_op jit(solution)/shard_map/ppermute | solution.py:206
  11.6 21.7 %collective-permute-start.1 = (bf16[2,3,256,256]{3,2,1,0:T(8,128)(2,1)}, bf16[2,3,256,256]{3,2,1,0:T(8,128)(2,1)S(1)}, u32[]{:S(2)}, u32[]{:S(2)}) collective-permute-start(bf16[2,3,256,256]{3,2,1,0:T(8,128)(2,1)} %get-tuple-element.22), channel_id=1, source_target_pairs={{0,2},{2,4},{4,6},{6,8},{8,10},{10,12},{12,14},{14,0},{1,3},{3,5},... | collective-permute-start | bytes 2359304 | tf_op jit(solution)/shard_map/ppermute | solution.py:206
  11.6 15.7 %copy-start.3 = (bf16[1024,256]{1,0:T(8,128)(2,1)S(1)}, bf16[1024,256]{1,0:T(8,128)(2,1)}, u32[]{:S(2)}) copy-start(bf16[1024,256]{1,0:T(8,128)(2,1)} %refs_6_.1) | copy-start | bytes 1572868
  16.7 44.6 %all-to-all-start = ((bf16[256,8,256]{2,1,0:T(8,128)(2,1)}), bf16[256,8,256]{2,1,0:T(8,128)(2,1)S(1)}, u32[]{:S(2)}, u32[]{:S(2)}) async-start(bf16[256,8,256]{2,1,0:T(8,128)(2,1)} %bitcast.25), calls=%async_computation | async-start | bytes 2097152 | tf_op jit(solution)/shard_map/all_to_all | solution.py:224
  27.3 3.8 %collective-permute-start.5 = (bf16[1024,256]{1,0:T(8,128)(2,1)S(1)}, bf16[1024,256]{1,0:T(8,128)(2,1)S(1)}, u32[]{:S(2)}, u32[]{:S(2)}) collective-permute-start(bf16[1024,256]{1,0:T(8,128)(2,1)S(1)} %copy-done.3), channel_id=1, source_target_pairs={{0,1},{1,0},{2,3},{3,2},{4,5},{5,4},{6,7},{7,6},{8,9},{9,8},{10,11... | collective-permute-start | bytes 1572872 | tf_op jit(solution)/shard_map/ppermute | solution.py:207
  29.5 2.3 %collective-permute-start.6 = (bf16[1024,256]{1,0:T(8,128)(2,1)}, bf16[1024,256]{1,0:T(8,128)(2,1)S(1)}, u32[]{:S(2)}, u32[]{:S(2)}) collective-permute-start(bf16[1024,256]{1,0:T(8,128)(2,1)} %refs_7_.1), channel_id=1, source_target_pairs={{0,1},{1,0},{2,3},{3,2},{4,5},{5,4},{6,7},{7,6},{8,9},{9,8},{10,11... | collective-permute-start | bytes 1572872 | tf_op jit(solution)/shard_map/ppermute | solution.py:207
  29.6 2.9 %collective-permute-start.7 = (bf16[1024,256]{1,0:T(8,128)(2,1)}, bf16[1024,256]{1,0:T(8,128)(2,1)S(1)}, u32[]{:S(2)}, u32[]{:S(2)}) collective-permute-start(bf16[1024,256]{1,0:T(8,128)(2,1)} %refs_8_.1), channel_id=1, source_target_pairs={{0,1},{1,0},{2,3},{3,2},{4,5},{5,4},{6,7},{7,6},{8,9},{9,8},{10,11... | collective-permute-start | bytes 1572872 | tf_op jit(solution)/shard_map/ppermute | solution.py:207
  31.1 1.5 %copy-start.5 = (bf16[1024,256]{1,0:T(8,128)(2,1)}, bf16[1024,256]{1,0:T(8,128)(2,1)S(1)}, u32[]{:S(2)}) copy-start(bf16[1024,256]{1,0:T(8,128)(2,1)S(1)} %collective-permute-done.5.refs_12_) | copy-start | bytes 1572868
  31.8 0.8 copy-start.6
  32.6 0.8 copy-start.7
  33.3 27.9 %copy-start.1 = (bf16[2,3,256,256]{3,2,1,0:T(8,128)(2,1)}, bf16[2,3,256,256]{3,2,1,0:T(8,128)(2,1)S(1)}, u32[]{:S(2)}) copy-start(bf16[2,3,256,256]{3,2,1,0:T(8,128)(2,1)S(1)} %collective-permute-done.refs_15_) | copy-start | bytes 2359300
  33.4 27.9 %copy-start.2 = (bf16[2,3,256,256]{3,2,1,0:T(8,128)(2,1)}, bf16[2,3,256,256]{3,2,1,0:T(8,128)(2,1)S(1)}, u32[]{:S(2)}) copy-start(bf16[2,3,256,256]{3,2,1,0:T(8,128)(2,1)S(1)} %collective-permute-done.1.refs_21_) | copy-start | bytes 2359300
  33.4 14.7 %collective-permute-start.8 = (bf16[3,256,256]{2,1,0:T(8,128)(2,1)S(1)}, bf16[3,256,256]{2,1,0:T(8,128)(2,1)}, u32[]{:S(2)}, u32[]{:S(2)}) collective-permute-start(bf16[3,256,256]{2,1,0:T(8,128)(2,1)S(1)} %get-tuple-element.34), channel_id=1, source_target_pairs={{0,64},{64,0},{128,192},{192,128},{1,65},{65,1},{129,193},{193,129... | collective-permute-start | bytes 1179656 | tf_op jit(solution)/shard_map/ppermute | solution.py:214
  33.5 25.4 %collective-permute-start.10 = (bf16[2,3,256,256]{3,2,1,0:T(8,128)(2,1)S(1)}, bf16[2,3,256,256]{3,2,1,0:T(8,128)(2,1)S(1)}, u32[]{:S(2)}, u32[]{:S(2)}) collective-permute-start(bf16[2,3,256,256]{3,2,1,0:T(8,128)(2,1)S(1)} %collective-permute-done.refs_15_), channel_id=1, source_target_pairs={{0,1},{1,0},{2,3},{3,2},{4,5},{5,4},{6,7},{7,6},{8,9},{9,8},{10,11... | collective-permute-start | bytes 2359304 | tf_op jit(solution)/shard_map/ppermute | solution.py:215
  37.7 17.9 %collective-permute-start.9 = (bf16[3,256,256]{2,1,0:T(8,128)(2,1)S(1)}, bf16[3,256,256]{2,1,0:T(8,128)(2,1)}, u32[]{:S(2)}, u32[]{:S(2)}) collective-permute-start(bf16[3,256,256]{2,1,0:T(8,128)(2,1)S(1)} %get-tuple-element.33), channel_id=1, source_target_pairs={{0,192},{192,0},{64,128},{128,64},{1,193},{193,1},{65,129},{129,65... | collective-permute-start | bytes 1179656 | tf_op jit(solution)/shard_map/ppermute | solution.py:214
  39.5 16.6 %collective-permute-start.13 = (bf16[3,256,256]{2,1,0:T(8,128)(2,1)S(1)}, bf16[3,256,256]{2,1,0:T(8,128)(2,1)}, u32[]{:S(2)}, u32[]{:S(2)}) collective-permute-start(bf16[3,256,256]{2,1,0:T(8,128)(2,1)S(1)} %get-tuple-element.32), channel_id=1, source_target_pairs={{0,16},{16,0},{32,48},{48,32},{1,17},{17,1},{33,49},{49,33},{2,18}... | collective-permute-start | bytes 1179656 | tf_op jit(solution)/shard_map/ppermute | solution.py:214
  40.9 17.1 %collective-permute-start.14 = (bf16[3,256,256]{2,1,0:T(8,128)(2,1)S(1)}, bf16[3,256,256]{2,1,0:T(8,128)(2,1)}, u32[]{:S(2)}, u32[]{:S(2)}) collective-permute-start(bf16[3,256,256]{2,1,0:T(8,128)(2,1)S(1)} %get-tuple-element.31), channel_id=1, source_target_pairs={{0,48},{48,0},{16,32},{32,16},{1,49},{49,1},{17,33},{33,17},{2,50}... | collective-permute-start | bytes 1179656 | tf_op jit(solution)/shard_map/ppermute | solution.py:214
  48.1 11.7 %collective-permute-start.15 = (bf16[2,3,256,256]{3,2,1,0:T(8,128)(2,1)S(1)}, bf16[2,3,256,256]{3,2,1,0:T(8,128)(2,1)}, u32[]{:S(2)}, u32[]{:S(2)}) collective-permute-start(bf16[2,3,256,256]{3,2,1,0:T(8,128)(2,1)S(1)} %collective-permute-done.1.refs_21_), channel_id=1, source_target_pairs={{0,1},{1,0},{2,3},{3,2},{4,5},{5,4},{6,7},{7,6},{8,9},{9,8},{10,11... | collective-permute-start | bytes 2359304 | tf_op jit(solution)/shard_map/ppermute | solution.py:215
  55.5 4.3 %collective-permute-start.11 = (bf16[3,256,256]{2,1,0:T(8,128)(2,1)}, bf16[3,256,256]{2,1,0:T(8,128)(2,1)}, u32[]{:S(2)}, u32[]{:S(2)}) collective-permute-start(bf16[3,256,256]{2,1,0:T(8,128)(2,1)} %collective-permute-done.8.refs_16_), channel_id=1, source_target_pairs={{0,1},{1,0},{2,3},{3,2},{4,5},{5,4},{6,7},{7,6},{8,9},{9,8},{10,11... | collective-permute-start | bytes 1179656 | tf_op jit(solution)/shard_map/ppermute | solution.py:216
  56.1 3.7 %collective-permute-start.12 = (bf16[3,256,256]{2,1,0:T(8,128)(2,1)}, bf16[3,256,256]{2,1,0:T(8,128)(2,1)}, u32[]{:S(2)}, u32[]{:S(2)}) collective-permute-start(bf16[3,256,256]{2,1,0:T(8,128)(2,1)} %collective-permute-done.9.refs_17_), channel_id=1, source_target_pairs={{0,1},{1,0},{2,3},{3,2},{4,5},{5,4},{6,7},{7,6},{8,9},{9,8},{10,11... | collective-permute-start | bytes 1179656 | tf_op jit(solution)/shard_map/ppermute | solution.py:216
  58.0 2.7 %collective-permute-start.16 = (bf16[3,256,256]{2,1,0:T(8,128)(2,1)}, bf16[3,256,256]{2,1,0:T(8,128)(2,1)}, u32[]{:S(2)}, u32[]{:S(2)}) collective-permute-start(bf16[3,256,256]{2,1,0:T(8,128)(2,1)} %collective-permute-done.13.refs_22_), channel_id=1, source_target_pairs={{0,1},{1,0},{2,3},{3,2},{4,5},{5,4},{6,7},{7,6},{8,9},{9,8},{10,11... | collective-permute-start | bytes 1179656 | tf_op jit(solution)/shard_map/ppermute | solution.py:216
  59.0 2.3 %copy-start.4 = (bf16[2,3,256,256]{3,2,1,0:T(8,128)(2,1)}, bf16[2,3,256,256]{3,2,1,0:T(8,128)(2,1)S(1)}, u32[]{:S(2)}) copy-start(bf16[2,3,256,256]{3,2,1,0:T(8,128)(2,1)S(1)} %collective-permute-done.10.refs_18_) | copy-start | bytes 2359300
  59.0 2.2 %collective-permute-start.17 = (bf16[3,256,256]{2,1,0:T(8,128)(2,1)}, bf16[3,256,256]{2,1,0:T(8,128)(2,1)}, u32[]{:S(2)}, u32[]{:S(2)}) collective-permute-start(bf16[3,256,256]{2,1,0:T(8,128)(2,1)} %collective-permute-done.14.refs_23_), channel_id=1, source_target_pairs={{0,1},{1,0},{2,3},{3,2},{4,5},{5,4},{6,7},{7,6},{8,9},{9,8},{10,11... | collective-permute-start | bytes 1179656 | tf_op jit(solution)/shard_map/ppermute | solution.py:216
  61.2 1.0 copy-start
where the time goes:
time: 118 us
  blocking collectives  37.7 us (32%)
  starting transfers between devices  36.4 us (31%)
  Pallas kernels  26.6 us (23%)
  waiting for transfers between devices  14.3 us (12%)
  local copies, waits for them, and re-layouts  1.86 us (2%)
  other arithmetic  1.18 us (1%)
    all_to_all x1, blocking collectives, local(): lax.all_to_all(sent.reshape(DEVS, OWN, COLS), ORDER, 0, 0, tiled=True)  37.7 us
    pallas_call x1, Pallas kernels, middle(): pl.pallas_call(body, out_shape=jax.ShapeDtypeStruct((GROUP, LOCAL, COLS),...  13.2 us
    all_to_all x1, starting transfers between devices, local(): got = lax.all_to_all(agg.reshape(DEVS, OWN, COLS), ORDER, 0, 0, tiled=True)  10.6 us
    ppermute x4, waiting for transfers between devices, local(): sides.append(lax.ppermute(far[g][sub], 'xy'[g], (even, odd)[sub]))  10.4 us
    pallas_call x2, Pallas kernels, hop(): pl.pallas_call(body, out_shape=jax.ShapeDtypeStruct((VERT, COLS), BF16),...  9.97 us
    ppermute x2, starting transfers between devices, local(): far_swap = lax.ppermute(far[g], 'core', swap)  7.97 us
    ppermute x6, starting transfers between devices, local(): swapped = [lax.ppermute(w, 'core', swap) for w in weights]  6.45 us
    ppermute x4, starting transfers between devices, local(): sides.append(lax.ppermute(far[g][sub], 'xy'[g], (even, odd)[sub]))  5.15 us
  transfers between devices with their start and end apart: 19, of which 8 were waited for; matrix products, arithmetic and copies ran while one was open for 1% of the time, Pallas kernels for 7%

commit v1 on v0

--- a/solution.py
+++ b/solution.py
@@ -62,14 +62,15 @@
     )(index, field, blocks)
 
 
-def middle_body(scale, own, bias, got, *refs):
+def middle_body(scale, bias, got, *refs):
     pieces, out = refs[:24], refs[24]
     w, hidden, query, keys, values, table, sems = refs[25:]
-    me = own[0]
+    me = lax.axis_index("zl") * 2 + lax.axis_index("core")
+    halves = (lax.axis_index("x") % 2, lax.axis_index("y") % 2)
     copies = []
     for i in range(6):
         group, j = i // 3, i % 3
-        half = own[1 + group]
+        half = halves[group]
         row = []
 
         def move(piece, block, start=None):
@@ -139,7 +140,7 @@
         out[g] = dot(keys[...], w[5, g]).astype(BF16)
 
 
-def middle(own, bias, got, pieces, scale):
+def middle(bias, got, pieces, scale):
     def body(*refs):
         middle_body(scale, *refs)
 
@@ -147,17 +148,18 @@
     return pl.pallas_call(
         body,
         out_shape=jax.ShapeDtypeStruct((GROUP, LOCAL, COLS), BF16),
-        in_specs=[pl.BlockSpec(memory_space=pltpu.SMEM), vmem, vmem]
+        in_specs=[vmem, vmem]
         + [pl.BlockSpec(memory_space=pl.ANY)] * 24,
         out_specs=vmem,
         scratch_shapes=[pltpu.VMEM((6, GROUP, FEAT, COLS), BF16)]
         + [pltpu.VMEM((LOCAL, FEAT), BF16)] * 4
         + [pltpu.VMEM((LOCAL, LOCAL), F32), pltpu.SemaphoreType.DMA((6, 10))],
         name="middle",
-    )(own, bias, got, *pieces)
-
-
-def pack_body(half, *refs):
+    )(bias, got, *pieces)
+
+
+def pack_body(*refs):
+    half = (lax.axis_index("x") % 2, lax.axis_index("y") % 2)
     inputs, outputs, sems = refs[:6], refs[6:8], refs[8]
     copies = []
     for i in range(6):
@@ -172,16 +174,16 @@
         copy.wait()
 
 
-def pack(half, weights):
+def pack(weights):
     anywhere = pl.BlockSpec(memory_space=pl.ANY)
     return pl.pallas_call(
         pack_body,
         out_shape=[jax.ShapeDtypeStruct((2, 3, QUART, COLS), BF16)] * 2,
-        in_specs=[pl.BlockSpec(memory_space=pltpu.SMEM)] + [anywhere] * 6,
+        in_specs=[anywhere] * 6,
         out_specs=[pl.BlockSpec(memory_space=pltpu.VMEM)] * 2,
         scratch_shapes=[pltpu.SemaphoreType.DMA((6, 2))],
         name="pack",
-    )(half, *weights)
+    )(*weights)
 
 
 def z_partner(up):
@@ -198,14 +200,12 @@
     scale = 1.0 / math.sqrt(FEAT)
     weights = (hop_in, query_w, key_w, value_w, output_w, hop_out)
     swap = [(0, 1), (1, 0)]
-    halves = jnp.stack([lax.axis_index("x") % 2, lax.axis_index("y") % 2]).astype(jnp.int32)
-    groups = pack(halves, weights)
+    groups = pack(weights)
     features, groups = lax.optimization_barrier((features, groups))
     far = []
     for g in range(2):
         far.append(lax.ppermute(groups[g], ("zh", "zl"), z_partner(g == 1)))
     swapped = [lax.ppermute(w, "core", swap) for w in weights]
-    far, swapped = lax.optimization_barrier((far, swapped))
     pieces = list(weights) + list(swapped)
     even, odd = [(0, 1), (1, 0), (2, 3), (3, 2)], [(0, 3), (3, 0), (1, 2), (2, 1)]
     for g in range(2):
@@ -217,12 +217,9 @@
         pieces += [far[g], *sides, far_swap, *side_swap]
     index = block_index[0].T
     blocks = block_values[0]
-    place = lax.axis_index("zl") * 2 + lax.axis_index("core")
-    own = jnp.concatenate([place.astype(jnp.int32).reshape(1), halves])
-
     agg = hop(features[0], index, blocks, False)
     got = lax.all_to_all(agg.reshape(DEVS, OWN, COLS), ORDER, 0, 0, tiled=True)
-    sent = middle(own, time_bias, got.reshape(GROUP, LOCAL, COLS), pieces, scale)
+    sent = middle(time_bias, got.reshape(GROUP, LOCAL, COLS), pieces, scale)
     back = lax.all_to_all(sent.reshape(DEVS, OWN, COLS), ORDER, 0, 0, tiled=True)
     return hop(back.reshape(VERT, COLS), index, blocks, True)[None]
 

time: 118 us -> 144 us (1.22)
  waiting for transfers between devices: 14.3 us -> 37.9 us
  starting transfers between devices: 36.4 us -> 38.9 us
    ppermute x2, waiting for transfers between devices: 0.01 us -> 31.5 us  [local(): far.append(lax.ppermute(groups[g], ('zh', 'zl'), z_partner(g == 1)))]
    ppermute x4, waiting for transfers between devices: 10.4 us -> 3.37 us  [local(): sides.append(lax.ppermute(far[g][sub], 'xy'[g], (even, odd)[sub]))]
    ppermute x2, starting transfers between devices: 7.97 us -> 1.93 us  [local(): far_swap = lax.ppermute(far[g], 'core', swap)]
    ppermute x2, starting transfers between devices: 3.95 us -> 8.03 us  [local(): far.append(lax.ppermute(groups[g], ('zh', 'zl'), z_partner(g == 1)))]
    ppermute x4, starting transfers between devices: 2.25 us -> 5.86 us  [local(): side_swap = [lax.ppermute(side, 'core', swap) for side in sides]]
    ppermute x4, starting transfers between devices: 5.15 us -> 7.16 us  [local(): sides.append(lax.ppermute(far[g][sub], 'xy'[g], (even, odd)[sub]))]
  transfers between devices with their start and end apart: 19 -> 19, of which waited for: 8 -> 7; matrix products, arithmetic and copies ran while one was open for 1% -> 0% of each run, Pallas kernels for 7% -> 4%
where the time goes in v1:
time: 144 us; the launch traced here: 143 us
  starting transfers between devices  38.9 us (27%)
  waiting for transfers between devices  37.9 us (26%)
  blocking collectives  37.9 us (26%)
  Pallas kernels  26 us (18%)
  local copies, waits for them, and re-layouts  2.45 us (2%)
    all_to_all x1, blocking collectives, local(): lax.all_to_all(sent.reshape(DEVS, OWN, COLS), ORDER, 0, 0, tiled=True)  37.9 us
    ppermute x2, waiting for transfers between devices, local(): far.append(lax.ppermute(groups[g], ('zh', 'zl'), z_partner(g == 1)))  31.5 us
    pallas_call x1, Pallas kernels, middle(): pl.pallas_call(body, out_shape=jax.ShapeDtypeStruct((GROUP, LOCAL, COLS),...  13.3 us
    pallas_call x2, Pallas kernels, hop(): pl.pallas_call(body, out_shape=jax.ShapeDtypeStruct((VERT, COLS), BF16),...  9.97 us
    all_to_all x1, starting transfers between devices, local(): got = lax.all_to_all(agg.reshape(DEVS, OWN, COLS), ORDER, 0, 0, tiled=True)  9.82 us
    ppermute x2, starting transfers between devices, local(): far.append(lax.ppermute(groups[g], ('zh', 'zl'), z_partner(g == 1)))  8.03 us
    ppermute x4, starting transfers between devices, local(): sides.append(lax.ppermute(far[g][sub], 'xy'[g], (even, odd)[sub]))  7.16 us
    ppermute x6, starting transfers between devices, local(): swapped = [lax.ppermute(w, 'core', swap) for w in weights]  6.14 us
  transfers between devices with their start and end apart: 19, of which 7 were waited for; matrix products, arithmetic and copies ran while one was open for 0% of the time, Pallas kernels for 4%

profile of v1, /device:TPU:1, one launch (start us, length us, event | category | flops | bytes accessed | tf_op | source)
XLA Modules:
  0.0 143.3 jit_solution(332276651704351234)
XLA Ops:
  0.0 2.7 %pack.1 = (bf16[2,3,256,256]{3,2,1,0:T(8,128)(2,1)}, bf16[2,3,256,256]{3,2,1,0:T(8,128)(2,1)}) custom-call(bf16[1024,256]{1,0:T(8,128)(2,1)} %refs_2_.3, bf16[1024,256]{1,0:T(8,128)(2,1)} %refs_3_.3, bf16[1024,256]{1,0:T(8,128)(2,1)} %refs_4_.3, bf16[1024,256]{1,0:T(8,128)(2,1)} %refs_5_.3, bf16[1024,256]{1,0:T(8,128)(2,1)} %refs_6_.1, bf16[1024,256]{1,0:T(8,128)(2,1)} %refs_7_.1), custom_call_target="tpu_custom_call" | custom-call | tf_op jit(solution)/shard_map/pack/pallas_call | solution.py:179
  2.7 6.5 %collective-permute-start.6 = (bf16[2,3,256,256]{3,2,1,0:T(8,128)(2,1)}, bf16[2,3,256,256]{3,2,1,0:T(8,128)(2,1)S(1)}, u32[]{:S(2)}, u32[]{:S(2)}) collective-permute-start(bf16[2,3,256,256]{3,2,1,0:T(8,128)(2,1)} %get-tuple-element.13), channel_id=1, source_target_pairs={{0,14},{2,0},{4,2},{6,4},{8,6},{10,8},{12,10},{14,12},{1,15},{3,1}... | collective-permute-start | bytes 2359304 | tf_op jit(solution)/shard_map/ppermute | solution.py:207
  9.2 5.0 %hop.1 = bf16[2048,256]{1,0:T(8,128)(2,1)} custom-call(s32[8,16]{1,0:T(8,128)} %bitcast.25, bf16[2048,256]{1,0:T(8,128)(2,1)} %bitcast.24, bf16[16,8,128,128]{3,2,1,0:T(8,128)(2,1)} %bitcast.18), custom_call_target="tpu_custom_call" | custom-call | tf_op jit(solution)/shard_map/hop/pallas_call | solution.py:49
  14.2 9.8 %all-to-all-start = ((bf16[256,8,256]{2,1,0:T(8,128)(2,1)}), bf16[256,8,256]{2,1,0:T(8,128)(2,1)S(1)}, u32[]{:S(2)}, u32[]{:S(2)}) async-start(bf16[256,8,256]{2,1,0:T(8,128)(2,1)} %bitcast.22), calls=%async_computation | async-start | bytes 2097152 | tf_op jit(solution)/shard_map/all_to_all | solution.py:221
  24.0 1.6 %collective-permute-start.12 = (bf16[2,3,256,256]{3,2,1,0:T(8,128)(2,1)}, bf16[2,3,256,256]{3,2,1,0:T(8,128)(2,1)S(1)}, u32[]{:S(2)}, u32[]{:S(2)}) collective-permute-start(bf16[2,3,256,256]{3,2,1,0:T(8,128)(2,1)} %get-tuple-element.14), channel_id=1, source_target_pairs={{0,2},{2,4},{4,6},{6,8},{8,10},{10,12},{12,14},{14,0},{1,3},{3,5},... | collective-permute-start | bytes 2359304 | tf_op jit(solution)/shard_map/ppermute | solution.py:207
  25.6 0.0 copy-done.3
  25.6 0.8 collective-permute-start
  26.4 0.1 collective-permute-start.1
  26.5 0.4 collective-permute-start.2
  26.9 1.0 collective-permute-done.refs_8_
  27.9 0.4 collective-permute-start.3
  28.3 0.4 collective-permute-done.1.refs_9_
  28.7 0.4 collective-permute-start.4
  29.0 0.0 collective-permute-done.6.refs_14_
  29.0 0.0 copy-done.5
  29.0 0.4 copy-done.6
  29.5 4.1 %collective-permute-start.5 = (bf16[1024,256]{1,0:T(8,128)(2,1)}, bf16[1024,256]{1,0:T(8,128)(2,1)S(1)}, u32[]{:S(2)}, u32[]{:S(2)}) collective-permute-start(bf16[1024,256]{1,0:T(8,128)(2,1)} %refs_7_.1), channel_id=1, source_target_pairs={{0,1},{1,0},{2,3},{3,2},{4,5},{5,4},{6,7},{7,6},{8,9},{9,8},{10,11... | collective-permute-start | bytes 1572872 | tf_op jit(solution)/shard_map/ppermute | solution.py:208
  33.6 0.1 slice_bitcast_fusion.2
  33.6 0.0 collective-permute-done.2.refs_10_
  33.7 0.0 copy-start.7
  33.7 1.5 %collective-permute-start.7 = (bf16[3,256,256]{2,1,0:T(8,128)(2,1)S(1)}, bf16[3,256,256]{2,1,0:T(8,128)(2,1)S(1)}, u32[]{:S(2)}, u32[]{:S(2)}) collective-permute-start(bf16[3,256,256]{2,1,0:T(8,128)(2,1)S(1)} %get-tuple-element.18), channel_id=1, source_target_pairs={{0,64},{64,0},{128,192},{192,128},{1,65},{65,1},{129,193},{193,129... | collective-permute-start | bytes 1179656 | tf_op jit(solution)/shard_map/ppermute | solution.py:214
  35.2 31.5 %collective-permute-done.12.refs_20_ = bf16[2,3,256,256]{3,2,1,0:T(8,128)(2,1)S(1)} collective-permute-done((bf16[2,3,256,256]{3,2,1,0:T(8,128)(2,1)}, bf16[2,3,256,256]{3,2,1,0:T(8,128)(2,1)S(1)}, u32[]{:S(2)}, u32[]{:S(2)}) %collective-permute-start.12) | collective-permute-done | bytes 786464 | tf_op jit(solution)/shard_map/ppermute | solution.py:207
  66.7 2.4 %collective-permute-start.8 = (bf16[3,256,256]{2,1,0:T(8,128)(2,1)S(1)}, bf16[3,256,256]{2,1,0:T(8,128)(2,1)S(1)}, u32[]{:S(2)}, u32[]{:S(2)}) collective-permute-start(bf16[3,256,256]{2,1,0:T(8,128)(2,1)S(1)} %get-tuple-element.17), channel_id=1, source_target_pairs={{0,192},{192,0},{64,128},{128,64},{1,193},{193,1},{65,129},{129,65... | collective-permute-start | bytes 1179656 | tf_op jit(solution)/shard_map/ppermute | solution.py:214
  69.1 0.1 slice_bitcast_fusion
  69.2 0.0 collective-permute-done.3.refs_11_
  69.2 0.0 copy-start.8
  69.2 1.3 collective-permute-start.13
  70.5 0.0 collective-permute-done.4.refs_12_
  70.5 1.9 %collective-permute-start.14 = (bf16[3,256,256]{2,1,0:T(8,128)(2,1)S(1)}, bf16[3,256,256]{2,1,0:T(8,128)(2,1)S(1)}, u32[]{:S(2)}, u32[]{:S(2)}) collective-permute-start(bf16[3,256,256]{2,1,0:T(8,128)(2,1)S(1)} %get-tuple-element.15), channel_id=1, source_target_pairs={{0,48},{48,0},{16,32},{32,16},{1,49},{49,1},{17,33},{33,17},{2,50}... | collective-permute-start | bytes 1179656 | tf_op jit(solution)/shard_map/ppermute | solution.py:214
  72.4 0.0 collective-permute-done.7.refs_15_
  72.4 1.8 %collective-permute-start.10 = (bf16[3,256,256]{2,1,0:T(8,128)(2,1)S(1)}, bf16[3,256,256]{2,1,0:T(8,128)(2,1)S(1)}, u32[]{:S(2)}, u32[]{:S(2)}) collective-permute-start(bf16[3,256,256]{2,1,0:T(8,128)(2,1)S(1)} %collective-permute-done.7.refs_15_), channel_id=1, source_target_pairs={{0,1},{1,0},{2,3},{3,2},{4,5},{5,4},{6,7},{7,6},{8,9},{9,8},{10,11... | collective-permute-start | bytes 1179656 | tf_op jit(solution)/shard_map/ppermute | solution.py:216
  74.2 0.0 collective-permute-done.5.refs_13_
  74.2 0.1 collective-permute-start.15
  74.3 3.3 %collective-permute-done.8.refs_16_ = bf16[3,256,256]{2,1,0:T(8,128)(2,1)S(1)} collective-permute-done((bf16[3,256,256]{2,1,0:T(8,128)(2,1)S(1)}, bf16[3,256,256]{2,1,0:T(8,128)(2,1)S(1)}, u32[]{:S(2)}, u32[]{:S(2)}) %collective-permute-start.8) | collective-permute-done | bytes 393248 | tf_op jit(solution)/shard_map/ppermute | solution.py:214
  77.6 1.8 %collective-permute-start.9 = (bf16[2,3,256,256]{3,2,1,0:T(8,128)(2,1)S(1)}, bf16[2,3,256,256]{3,2,1,0:T(8,128)(2,1)}, u32[]{:S(2)}, u32[]{:S(2)}) collective-permute-start(bf16[2,3,256,256]{3,2,1,0:T(8,128)(2,1)S(1)} %collective-permute-done.6.refs_14_), channel_id=1, source_target_pairs={{0,1},{1,0},{2,3},{3,2},{4,5},{5,4},{6,7},{7,6},{8,9},{9,8},{10,11... | collective-permute-start | bytes 2359304 | tf_op jit(solution)/shard_map/ppermute | solution.py:215
  79.4 0.0 collective-permute-done.13.refs_21_
  79.4 1.4 collective-permute-start.11
  80.8 0.1 collective-permute-done.14.refs_22_
  80.9 2.4 %collective-permute-start.16 = (bf16[3,256,256]{2,1,0:T(8,128)(2,1)S(1)}, bf16[3,256,256]{2,1,0:T(8,128)(2,1)S(1)}, u32[]{:S(2)}, u32[]{:S(2)}) collective-permute-start(bf16[3,256,256]{2,1,0:T(8,128)(2,1)S(1)} %collective-permute-done.13.refs_21_), channel_id=1, source_target_pairs={{0,1},{1,0},{2,3},{3,2},{4,5},{5,4},{6,7},{7,6},{8,9},{9,8},{10,11... | collective-permute-start | bytes 1179656 | tf_op jit(solution)/shard_map/ppermute | solution.py:216
  83.3 0.0 collective-permute-done.10.refs_18_
  83.3 0.3 collective-permute-start.17
  83.6 0.0 collective-permute-done.11.refs_19_
  83.6 1.1 collective-permute-done.16.refs_24_
  84.6 0.6 collective-permute-done.17.refs_25_
  85.2 0.0 collective-permute-done.15.refs_23_
  85.2 0.0 copy-done.7
  85.2 0.0 copy-done.8
  85.2 0.0 copy-done.9
  85.2 0.0 copy-done.11
  85.2 0.0 copy-done.10
  85.2 0.0 copy-done.12
  85.2 0.0 copy-done.13
  85.3 0.0 copy-done.14
  85.3 0.0 copy-done.15
  85.3 0.1 copy-done.17
  85.4 0.5 copy-done.18
  85.9 0.0 collective-permute-done.9.refs_17_
  86.0 0.0 all-to-all-done
  86.0 0.0 copy-start
  86.0 0.8 copy-done.4
  86.8 0.3 copy-done
  87.2 13.3 %middle.1 = bf16[4,512,256]{2,1,0:T(8,128)(2,1)} custom-call(f32[64,64]{1,0:T(8,128)} %refs_0_.3, bf16[4,512,256]{2,1,0:T(8,128)(2,1)} %bitcast.20, bf16[1024,256]{1,0:T(8,128)(2,1)} %refs_2_.3, bf16[1024,256]{1,0:T(8,128)(2,1)} %refs_3_.3, bf16[1024,256]{1,0:T(8,128)(2,1)} %refs_4_.3, bf16[1024,256]{1,0:T(8,128)(2,1)} %refs_5_.3, ...), custom_call_target="tpu_custom_call" | custom-call | tf_op jit(solution)/shard_map/middle/pallas_call | solution.py:148
  100.5 37.9 %all_to_all.10 = bf16[256,8,256]{2,1,0:T(8,128)(2,1)} all-to-all(bf16[256,8,256]{2,1,0:T(8,128)(2,1)} %bitcast.21), channel_id=1, replica_groups=mesh['x'=4,'y'=4,'zh'=4,'zl'=2,'core'=2] {'zl','core','x','y','zh'}, dimensions={0} | all-to-all | bytes 2097152 | tf_op jit(solution)/shard_map/all_to_all | solution.py:223
  138.4 4.9 %hop_relu.1 = bf16[2048,256]{1,0:T(8,128)(2,1)} custom-call(s32[8,16]{1,0:T(8,128)} %bitcast.26, bf16[2048,256]{1,0:T(8,128)(2,1)} %bitcast.23, bf16[16,8,128,128]{3,2,1,0:T(8,128)(2,1)} %bitcast.19), custom_call_target="tpu_custom_call" | custom-call | tf_op jit(solution)/shard_map/hop_relu/pallas_call | solution.py:49
  (19 shorter events, 0.0 us)
Async XLA Ops:
  2.7 26.3 %collective-permute-start.6 = (bf16[2,3,256,256]{3,2,1,0:T(8,128)(2,1)}, bf16[2,3,256,256]{3,2,1,0:T(8,128)(2,1)S(1)}, u32[]{:S(2)}, u32[]{:S(2)}) collective-permute-start(bf16[2,3,256,256]{3,2,1,0:T(8,128)(2,1)} %get-tuple-element.13), channel_id=1, source_target_pairs={{0,14},{2,0},{4,2},{6,4},{8,6},{10,8},{12,10},{14,12},{1,15},{3,1}... | collective-permute-start | bytes 2359304 | tf_op jit(solution)/shard_map/ppermute | solution.py:207
  9.2 16.4 %copy-start.3 = (bf16[1024,256]{1,0:T(8,128)(2,1)S(1)}, bf16[1024,256]{1,0:T(8,128)(2,1)}, u32[]{:S(2)}) copy-start(bf16[1024,256]{1,0:T(8,128)(2,1)} %refs_2_.3) | copy-start | bytes 1572868
  14.2 71.7 %all-to-all-start = ((bf16[256,8,256]{2,1,0:T(8,128)(2,1)}), bf16[256,8,256]{2,1,0:T(8,128)(2,1)S(1)}, u32[]{:S(2)}, u32[]{:S(2)}) async-start(bf16[256,8,256]{2,1,0:T(8,128)(2,1)} %bitcast.22), calls=%async_computation | async-start | bytes 2097152 | tf_op jit(solution)/shard_map/all_to_all | solution.py:221
  24.0 42.6 %collective-permute-start.12 = (bf16[2,3,256,256]{3,2,1,0:T(8,128)(2,1)}, bf16[2,3,256,256]{3,2,1,0:T(8,128)(2,1)S(1)}, u32[]{:S(2)}, u32[]{:S(2)}) collective-permute-start(bf16[2,3,256,256]{3,2,1,0:T(8,128)(2,1)} %get-tuple-element.14), channel_id=1, source_target_pairs={{0,2},{2,4},{4,6},{6,8},{8,10},{10,12},{12,14},{14,0},{1,3},{3,5},... | collective-permute-start | bytes 2359304 | tf_op jit(solution)/shard_map/ppermute | solution.py:207
  25.6 2.3 %collective-permute-start = (bf16[1024,256]{1,0:T(8,128)(2,1)S(1)}, bf16[1024,256]{1,0:T(8,128)(2,1)S(1)}, u32[]{:S(2)}, u32[]{:S(2)}) collective-permute-start(bf16[1024,256]{1,0:T(8,128)(2,1)S(1)} %copy-done.3), channel_id=1, source_target_pairs={{0,1},{1,0},{2,3},{3,2},{4,5},{5,4},{6,7},{7,6},{8,9},{9,8},{10,11... | collective-permute-start | bytes 1572872 | tf_op jit(solution)/shard_map/ppermute | solution.py:208
  26.4 2.3 %collective-permute-start.1 = (bf16[1024,256]{1,0:T(8,128)(2,1)}, bf16[1024,256]{1,0:T(8,128)(2,1)S(1)}, u32[]{:S(2)}, u32[]{:S(2)}) collective-permute-start(bf16[1024,256]{1,0:T(8,128)(2,1)} %refs_3_.3), channel_id=1, source_target_pairs={{0,1},{1,0},{2,3},{3,2},{4,5},{5,4},{6,7},{7,6},{8,9},{9,8},{10,11... | collective-permute-start | bytes 1572872 | tf_op jit(solution)/shard_map/ppermute | solution.py:208
  26.5 7.2 %collective-permute-start.2 = (bf16[1024,256]{1,0:T(8,128)(2,1)}, bf16[1024,256]{1,0:T(8,128)(2,1)S(1)}, u32[]{:S(2)}, u32[]{:S(2)}) collective-permute-start(bf16[1024,256]{1,0:T(8,128)(2,1)} %refs_4_.3), channel_id=1, source_target_pairs={{0,1},{1,0},{2,3},{3,2},{4,5},{5,4},{6,7},{7,6},{8,9},{9,8},{10,11... | collective-permute-start | bytes 1572872 | tf_op jit(solution)/shard_map/ppermute | solution.py:208
  27.9 1.1 copy-start.5
  27.9 41.3 %collective-permute-start.3 = (bf16[1024,256]{1,0:T(8,128)(2,1)}, bf16[1024,256]{1,0:T(8,128)(2,1)S(1)}, u32[]{:S(2)}, u32[]{:S(2)}) collective-permute-start(bf16[1024,256]{1,0:T(8,128)(2,1)} %refs_5_.3), channel_id=1, source_target_pairs={{0,1},{1,0},{2,3},{3,2},{4,5},{5,4},{6,7},{7,6},{8,9},{9,8},{10,11... | collective-permute-start | bytes 1572872 | tf_op jit(solution)/shard_map/ppermute | solution.py:208
  28.7 0.8 copy-start.6
  28.7 41.9 %collective-permute-start.4 = (bf16[1024,256]{1,0:T(8,128)(2,1)}, bf16[1024,256]{1,0:T(8,128)(2,1)S(1)}, u32[]{:S(2)}, u32[]{:S(2)}) collective-permute-start(bf16[1024,256]{1,0:T(8,128)(2,1)} %refs_6_.1), channel_id=1, source_target_pairs={{0,1},{1,0},{2,3},{3,2},{4,5},{5,4},{6,7},{7,6},{8,9},{9,8},{10,11... | collective-permute-start | bytes 1572872 | tf_op jit(solution)/shard_map/ppermute | solution.py:208
  29.5 56.5 %copy-start.1 = (bf16[2,3,256,256]{3,2,1,0:T(8,128)(2,1)}, bf16[2,3,256,256]{3,2,1,0:T(8,128)(2,1)S(1)}, u32[]{:S(2)}) copy-start(bf16[2,3,256,256]{3,2,1,0:T(8,128)(2,1)S(1)} %collective-permute-done.6.refs_14_) | copy-start | bytes 2359300
  29.5 44.7 %collective-permute-start.5 = (bf16[1024,256]{1,0:T(8,128)(2,1)}, bf16[1024,256]{1,0:T(8,128)(2,1)S(1)}, u32[]{:S(2)}, u32[]{:S(2)}) collective-permute-start(bf16[1024,256]{1,0:T(8,128)(2,1)} %refs_7_.1), channel_id=1, source_target_pairs={{0,1},{1,0},{2,3},{3,2},{4,5},{5,4},{6,7},{7,6},{8,9},{9,8},{10,11... | collective-permute-start | bytes 1572872 | tf_op jit(solution)/shard_map/ppermute | solution.py:208
  33.7 51.5 %copy-start.7 = (bf16[1024,256]{1,0:T(8,128)(2,1)}, bf16[1024,256]{1,0:T(8,128)(2,1)S(1)}, u32[]{:S(2)}) copy-start(bf16[1024,256]{1,0:T(8,128)(2,1)S(1)} %collective-permute-done.2.refs_10_) | copy-start | bytes 1572868
  33.7 38.7 %collective-permute-start.7 = (bf16[3,256,256]{2,1,0:T(8,128)(2,1)S(1)}, bf16[3,256,256]{2,1,0:T(8,128)(2,1)S(1)}, u32[]{:S(2)}, u32[]{:S(2)}) collective-permute-start(bf16[3,256,256]{2,1,0:T(8,128)(2,1)S(1)} %get-tuple-element.18), channel_id=1, source_target_pairs={{0,64},{64,0},{128,192},{192,128},{1,65},{65,1},{129,193},{193,129... | collective-permute-start | bytes 1179656 | tf_op jit(solution)/shard_map/ppermute | solution.py:214
  66.7 19.3 %copy-start.2 = (bf16[2,3,256,256]{3,2,1,0:T(8,128)(2,1)}, bf16[2,3,256,256]{3,2,1,0:T(8,128)(2,1)S(1)}, u32[]{:S(2)}) copy-start(bf16[2,3,256,256]{3,2,1,0:T(8,128)(2,1)S(1)} %collective-permute-done.12.refs_20_) | copy-start | bytes 2359300
  66.7 10.9 %collective-permute-start.8 = (bf16[3,256,256]{2,1,0:T(8,128)(2,1)S(1)}, bf16[3,256,256]{2,1,0:T(8,128)(2,1)S(1)}, u32[]{:S(2)}, u32[]{:S(2)}) collective-permute-start(bf16[3,256,256]{2,1,0:T(8,128)(2,1)S(1)} %get-tuple-element.17), channel_id=1, source_target_pairs={{0,192},{192,0},{64,128},{128,64},{1,193},{193,1},{65,129},{129,65... | collective-permute-start | bytes 1179656 | tf_op jit(solution)/shard_map/ppermute | solution.py:214
  69.2 16.0 %copy-start.8 = (bf16[1024,256]{1,0:T(8,128)(2,1)}, bf16[1024,256]{1,0:T(8,128)(2,1)S(1)}, u32[]{:S(2)}) copy-start(bf16[1024,256]{1,0:T(8,128)(2,1)S(1)} %collective-permute-done.3.refs_11_) | copy-start | bytes 1572868
  69.2 10.2 %collective-permute-start.13 = (bf16[3,256,256]{2,1,0:T(8,128)(2,1)S(1)}, bf16[3,256,256]{2,1,0:T(8,128)(2,1)S(1)}, u32[]{:S(2)}, u32[]{:S(2)}) collective-permute-start(bf16[3,256,256]{2,1,0:T(8,128)(2,1)S(1)} %get-tuple-element.16), channel_id=1, source_target_pairs={{0,16},{16,0},{32,48},{48,32},{1,17},{17,1},{33,49},{49,33},{2,18}... | collective-permute-start | bytes 1179656 | tf_op jit(solution)/shard_map/ppermute | solution.py:214
  70.5 14.7 %copy-start.9 = (bf16[1024,256]{1,0:T(8,128)(2,1)}, bf16[1024,256]{1,0:T(8,128)(2,1)S(1)}, u32[]{:S(2)}) copy-start(bf16[1024,256]{1,0:T(8,128)(2,1)S(1)} %collective-permute-done.4.refs_12_) | copy-start | bytes 1572868
  70.5 10.4 %collective-permute-start.14 = (bf16[3,256,256]{2,1,0:T(8,128)(2,1)S(1)}, bf16[3,256,256]{2,1,0:T(8,128)(2,1)S(1)}, u32[]{:S(2)}, u32[]{:S(2)}) collective-permute-start(bf16[3,256,256]{2,1,0:T(8,128)(2,1)S(1)} %get-tuple-element.15), channel_id=1, source_target_pairs={{0,48},{48,0},{16,32},{32,16},{1,49},{49,1},{17,33},{33,17},{2,50}... | collective-permute-start | bytes 1179656 | tf_op jit(solution)/shard_map/ppermute | solution.py:214
  72.4 12.8 %copy-start.11 = (bf16[3,256,256]{2,1,0:T(8,128)(2,1)}, bf16[3,256,256]{2,1,0:T(8,128)(2,1)S(1)}, u32[]{:S(2)}) copy-start(bf16[3,256,256]{2,1,0:T(8,128)(2,1)S(1)} %collective-permute-done.7.refs_15_) | copy-start | bytes 1179652
  72.4 10.9 %collective-permute-start.10 = (bf16[3,256,256]{2,1,0:T(8,128)(2,1)S(1)}, bf16[3,256,256]{2,1,0:T(8,128)(2,1)S(1)}, u32[]{:S(2)}, u32[]{:S(2)}) collective-permute-start(bf16[3,256,256]{2,1,0:T(8,128)(2,1)S(1)} %collective-permute-done.7.refs_15_), channel_id=1, source_target_pairs={{0,1},{1,0},{2,3},{3,2},{4,5},{5,4},{6,7},{7,6},{8,9},{9,8},{10,11... | collective-permute-start | bytes 1179656 | tf_op jit(solution)/shard_map/ppermute | solution.py:216
  74.2 11.0 %copy-start.10 = (bf16[1024,256]{1,0:T(8,128)(2,1)}, bf16[1024,256]{1,0:T(8,128)(2,1)S(1)}, u32[]{:S(2)}) copy-start(bf16[1024,256]{1,0:T(8,128)(2,1)S(1)} %collective-permute-done.5.refs_13_) | copy-start | bytes 1572868
  74.2 11.0 %collective-permute-start.15 = (bf16[2,3,256,256]{3,2,1,0:T(8,128)(2,1)S(1)}, bf16[2,3,256,256]{3,2,1,0:T(8,128)(2,1)S(1)}, u32[]{:S(2)}, u32[]{:S(2)}) collective-permute-start(bf16[2,3,256,256]{3,2,1,0:T(8,128)(2,1)S(1)} %collective-permute-done.12.refs_20_), channel_id=1, source_target_pairs={{0,1},{1,0},{2,3},{3,2},{4,5},{5,4},{6,7},{7,6},{8,9},{9,8},{10,11... | collective-permute-start | bytes 2359304 | tf_op jit(solution)/shard_map/ppermute | solution.py:215
  77.6 7.6 %copy-start.12 = (bf16[3,256,256]{2,1,0:T(8,128)(2,1)}, bf16[3,256,256]{2,1,0:T(8,128)(2,1)S(1)}, u32[]{:S(2)}) copy-start(bf16[3,256,256]{2,1,0:T(8,128)(2,1)S(1)} %collective-permute-done.8.refs_16_) | copy-start | bytes 1179652
  77.6 8.4 %collective-permute-start.9 = (bf16[2,3,256,256]{3,2,1,0:T(8,128)(2,1)S(1)}, bf16[2,3,256,256]{3,2,1,0:T(8,128)(2,1)}, u32[]{:S(2)}, u32[]{:S(2)}) collective-permute-start(bf16[2,3,256,256]{3,2,1,0:T(8,128)(2,1)S(1)} %collective-permute-done.6.refs_14_), channel_id=1, source_target_pairs={{0,1},{1,0},{2,3},{3,2},{4,5},{5,4},{6,7},{7,6},{8,9},{9,8},{10,11... | collective-permute-start | bytes 2359304 | tf_op jit(solution)/shard_map/ppermute | solution.py:215
  79.4 5.8 %copy-start.13 = (bf16[3,256,256]{2,1,0:T(8,128)(2,1)}, bf16[3,256,256]{2,1,0:T(8,128)(2,1)S(1)}, u32[]{:S(2)}) copy-start(bf16[3,256,256]{2,1,0:T(8,128)(2,1)S(1)} %collective-permute-done.13.refs_21_) | copy-start | bytes 1179652
  79.4 4.1 %collective-permute-start.11 = (bf16[3,256,256]{2,1,0:T(8,128)(2,1)S(1)}, bf16[3,256,256]{2,1,0:T(8,128)(2,1)S(1)}, u32[]{:S(2)}, u32[]{:S(2)}) collective-permute-start(bf16[3,256,256]{2,1,0:T(8,128)(2,1)S(1)} %collective-permute-done.8.refs_16_), channel_id=1, source_target_pairs={{0,1},{1,0},{2,3},{3,2},{4,5},{5,4},{6,7},{7,6},{8,9},{9,8},{10,11... | collective-permute-start | bytes 1179656 | tf_op jit(solution)/shard_map/ppermute | solution.py:216
  80.9 4.4 %copy-start.14 = (bf16[3,256,256]{2,1,0:T(8,128)(2,1)}, bf16[3,256,256]{2,1,0:T(8,128)(2,1)S(1)}, u32[]{:S(2)}) copy-start(bf16[3,256,256]{2,1,0:T(8,128)(2,1)S(1)} %collective-permute-done.14.refs_22_) | copy-start | bytes 1179652
  80.9 3.7 %collective-permute-start.16 = (bf16[3,256,256]{2,1,0:T(8,128)(2,1)S(1)}, bf16[3,256,256]{2,1,0:T(8,128)(2,1)S(1)}, u32[]{:S(2)}, u32[]{:S(2)}) collective-permute-start(bf16[3,256,256]{2,1,0:T(8,128)(2,1)S(1)} %collective-permute-done.13.refs_21_), channel_id=1, source_target_pairs={{0,1},{1,0},{2,3},{3,2},{4,5},{5,4},{6,7},{7,6},{8,9},{9,8},{10,11... | collective-permute-start | bytes 1179656 | tf_op jit(solution)/shard_map/ppermute | solution.py:216
  83.3 2.0 %copy-start.15 = (bf16[3,256,256]{2,1,0:T(8,128)(2,1)}, bf16[3,256,256]{2,1,0:T(8,128)(2,1)S(1)}, u32[]{:S(2)}) copy-start(bf16[3,256,256]{2,1,0:T(8,128)(2,1)S(1)} %collective-permute-done.10.refs_18_) | copy-start | bytes 1179652
  83.3 1.9 %collective-permute-start.17 = (bf16[3,256,256]{2,1,0:T(8,128)(2,1)S(1)}, bf16[3,256,256]{2,1,0:T(8,128)(2,1)S(1)}, u32[]{:S(2)}, u32[]{:S(2)}) collective-permute-start(bf16[3,256,256]{2,1,0:T(8,128)(2,1)S(1)} %collective-permute-done.14.refs_22_), channel_id=1, source_target_pairs={{0,1},{1,0},{2,3},{3,2},{4,5},{5,4},{6,7},{7,6},{8,9},{9,8},{10,11... | collective-permute-start | bytes 1179656 | tf_op jit(solution)/shard_map/ppermute | solution.py:216
  83.6 1.7 %copy-start.16 = (bf16[3,256,256]{2,1,0:T(8,128)(2,1)}, bf16[3,256,256]{2,1,0:T(8,128)(2,1)S(1)}, u32[]{:S(2)}) copy-start(bf16[3,256,256]{2,1,0:T(8,128)(2,1)S(1)} %collective-permute-done.11.refs_19_) | copy-start | bytes 1179652
  84.6 0.8 copy-start.17
  85.2 0.8 copy-start.18
  85.9 0.9 copy-start.4
  86.0 1.2 copy-start
